TPU v7x, 256 devices: a whole 4x4x8 slice. The times are simulated.
256 devices in a mesh: seq: 32 (over x, z_hi, core), tp: 8 (over z_lo, y).
Axes of the slice: x: 4, y: 4, z: 8 (z_hi: 4, z_lo: 2; z = z_hi * 2 + z_lo), core: 2. Of those that a mesh axis runs over, the one named last changes fastest.
Arguments:
- tokens: bfloat16 [1024, 8192], P('tp', 'seq'), may hold values from -6 to 6
- gate_weight: bfloat16 [8192, 14336], P('seq', 'tp'), may hold values from -0.0625 to 0.0625
- up_weight: bfloat16 [8192, 14336], P('seq', 'tp'), may hold values from -0.0625 to 0.0625
- down_weight: bfloat16 [14336, 8192], P('tp', 'seq'), may hold values from -0.09375 to 0.09375
- masks: int32 [8, 112], P(None, 'tp'), may hold values from 0 to 1, as said below
- cotangent: bfloat16 [1024, 8192], P('tp', 'seq'), may hold values from -6 to 6
Outputs:
- output: bfloat16 [1024, 8192], P('tp', 'seq')
- grad_tokens: bfloat16 [1024, 8192], P('tp', 'seq')
- grad_gate: float32 [8192, 14336], P('seq', 'tp')
- grad_up: float32 [8192, 14336], P('seq', 'tp')
- grad_down: float32 [14336, 8192], P('tp', 'seq')
Inputs may be any that keep to these rules, and one draw needn't show every extreme that they name: Each row of masks holds exactly 28 ones. Cut a row into 8 groups of 14 consecutive blocks: in every row one group holds exactly 7 ones, and the remaining ones are spread over the other groups as evenly as possible, so that their counts differ by at most one.
All inputs are finite; a program needn't handle non-finite values.
Results may differ from a plain program's by a relative error of at most 0.0049.
Values may be sent and summed in bfloat16 or wider, within the bound.
No kernel may reach another device: no remote copies, remote signals or barrier semaphores. Data moves between devices by JAX's collectives and lax.ppermute only.
A program may use at most 128 MiB of HBM per device.

v0:
```python
import functools

import jax
import jax.numpy as jnp
from jax import lax
from jax.experimental import pallas as pl
from jax.experimental.pallas import tpu as pltpu
from jax.sharding import Mesh, PartitionSpec as P

BLK = 128
ROWBLK = 128
BASE = 3
EXTRA = 4
ROOM = (2, 3, 8)
SEQ = ("x", "zh", "core")
TP = ("zl", "y")
BF16 = jnp.bfloat16
F32 = jnp.float32
ANY = pl.BlockSpec(memory_space=pl.ANY)
VMEM = pl.BlockSpec(memory_space=pltpu.VMEM)
SMEM = pl.BlockSpec(memory_space=pltpu.SMEM)
PARAMS = pltpu.CompilerParams(vmem_limit_bytes=40 << 20)


def nt(a, b):
    return lax.dot_general(a, b, (((1,), (1,)), ((), ())), preferred_element_type=F32)


def nn(a, b):
    return jnp.dot(a, b, preferred_element_type=F32)


def tile(i):
    if isinstance(i, int):
        return pl.ds(i * BLK, BLK)
    return pl.ds(pl.multiple_of(i * BLK, BLK), BLK)


class Table:
    def __init__(self, rows, blocks):
        self.rows, self.blocks = rows, blocks
        self.base = 0
        self.extra = self.base + BASE * rows
        self.unit_row = self.extra + EXTRA * rows
        self.row_unit = self.unit_row + rows
        self.live_row = self.row_unit + rows
        self.live_at = self.live_row + rows * blocks
        self.live = self.live_at + rows * blocks
        self.spare = self.live + blocks
        self.size = self.spare + 1
        self.pairs = (BASE + EXTRA) * rows


def payload_kernel(blocks_kept, masks, tokens, cotangent, out):
    rows, feat = tokens.shape
    heavy = jnp.int32(0)
    for r in range(masks.shape[0]):
        kept = sum(masks[r, b] for b in range(masks.shape[1]))
        heavy += (kept > blocks_kept).astype(jnp.int32)
    count = jnp.full((out.shape[1] - rows, out.shape[2]), heavy.astype(F32)).astype(out.dtype)
    for k in range(out.shape[0]):
        out[k, :rows, :feat] = tokens[...]
        out[k, :rows, feat:] = cotangent[...]
        out[k, rows:, :] = count


def table_kernel(t, masks, out):
    for k in range(t.extra, t.row_unit):
        out[k] = 0
    for k in range(t.rows * t.blocks):
        out[t.live_row + k] = 0
        out[t.live_at + k] = t.pairs

    def row(r, c):
        units, live = c[0], list(c[1:])
        count = jnp.int32(0)
        for b in range(t.blocks):
            one = masks[r, b]
            kept, based = one == 1, count < BASE
            at = jnp.where(based, BASE * r, BASE * (t.rows - 1) + EXTRA * units) + count
            out[jnp.where(kept, t.base + at, t.spare)] = b
            out[jnp.where(kept, t.live_row + t.rows * b + live[b], t.spare)] = r
            out[jnp.where(kept, t.live_at + t.rows * b + live[b], t.spare)] = at
            live[b] += one
            count += one
        heavy = count > BASE
        out[t.row_unit + r] = jnp.where(heavy, units, -1)
        out[jnp.where(heavy, t.unit_row + units, t.spare)] = r
        return units + heavy.astype(jnp.int32), *live

    _, *live = lax.fori_loop(0, t.rows, row, (jnp.int32(0),) * (t.blocks + 1))
    for b in range(t.blocks):
        out[t.live + b] = live[b]


def partials_kernel(t, units, feat, place, table, own, other, gate_own, gate_other, up_own, up_other, down_own,
                    down_other, out):
    core = place[0]
    base, extra = BASE * t.rows // 2, EXTRA * units // 2

    def products(i, row, block):
        cols = tile(block)
        act = nn(own[row, :ROWBLK, :feat], jnp.concatenate([gate_own[:, cols], up_own[:, cols]], axis=1))
        act += nn(other[row, :ROWBLK, :feat], jnp.concatenate([gate_other[:, cols], up_other[:, cols]], axis=1))
        grad = nt(own[row, :ROWBLK, feat:], down_own[cols, :]) + nt(other[row, :ROWBLK, feat:], down_other[cols, :])
        out[tile(i), : 2 * BLK] = act.astype(out.dtype)
        out[tile(i), 2 * BLK :] = grad.astype(out.dtype)

    def some_base(n, c):
        for j in range(2 * BASE):
            i = n * 2 * BASE + j
            products(i, core * (t.rows // 2) + n * 2 + j // BASE, table[t.base + core * base + i])
        return c

    def some_extra(n, c):
        for j in range(2):
            i = n * 2 + j
            k = core * extra + i
            products(base + i, table[t.unit_row + k // EXTRA], table[t.extra + k])
        return c

    narrow = units < t.rows
    lax.fori_loop(0, base // (2 * BASE), some_base, 0, unroll=narrow)
    lax.fori_loop(0, extra // 2, some_extra, 0, unroll=narrow)


def listed(t, units, at):
    base, extra = BASE * t.rows // 2, EXTRA * units // 2
    e = at - 2 * base
    in_base = at + jnp.where(at >= base, extra, 0)
    return jnp.where(e < 0, in_base, base + e + jnp.where(e >= extra, base, 0))


def load_acts(t, units, place, blocks, acts, sems):
    quarter = (BASE * t.rows + EXTRA * units) * BLK // 8
    core, x = place[0], place[1]
    moves = []
    for k, whose in enumerate((core, 1 - core)):
        own, near, far = blocks[3 * k : 3 * k + 3]
        for ref, skip, d in ((own, 0, 0), (near, 0, 3), (near, quarter, 1), (far, 0, 2)):
            start = pl.multiple_of((4 * whose + (x + d) % 4) * quarter, 16)
            source, target = ref.at[pl.ds(skip, quarter)], acts.at[pl.ds(start, quarter)]
            moves.append(pltpu.make_async_copy(source, target, sems.at[len(moves)]))
    for move in moves:
        move.start()
    for move in moves:
        move.wait()


def rows_kernel(t, units, place, table, *refs):
    halves, (gate, up, down, out, acts, total, done, sems) = refs[:6], refs[6:]
    feat = down.shape[1]
    load_acts(t, units, place, halves, acts, sems)

    def products(at, picks):
        fwd, bwd = 0.0, 0.0
        for j, b in enumerate(picks):
            act, cols = acts[tile(listed(t, units, at + j)), :], tile(b)
            fwd += nn(act[:, :BLK], down[cols, :])
            bwd += nt(act[:, BLK:], jnp.concatenate([gate[:, cols], up[:, cols]], axis=1))
        return fwd, bwd

    def row(r, c):
        fwd, bwd = products(BASE * r, [table[t.base + BASE * r + j] for j in range(BASE)])
        total[:, :feat] = fwd
        total[:, feat:] = bwd
        u = table[t.row_unit + r]

        @pl.when(u >= 0)
        def _():
            fwd, bwd = products(BASE * t.rows + EXTRA * u, [table[t.extra + EXTRA * u + j] for j in range(EXTRA)])
            total[:, :feat] += fwd
            total[:, feat:] += bwd

        done[tile(r), :] = total[...].astype(done.dtype)
        pltpu.make_async_copy(done.at[tile(r)], out.at[tile(r)], sems.at[8]).start()
        return c

    lax.fori_loop(0, t.rows, row, 0, unroll=2 if units < t.rows else 1)
    pltpu.make_async_copy(done, out, sems.at[8]).wait()


def weights_kernel(t, units, together, scale, place, table, *refs):
    halves, (rows, grad_gate, grad_up, grad_down, acts, turned, sems) = refs[:6], refs[6:]
    feat = grad_down.shape[1]
    step = pl.program_id(0)

    @pl.when(step == 0)
    def _():
        load_acts(t, units, place, halves, acts, sems)
        acts[tile(t.pairs), :] = jnp.zeros((BLK, acts.shape[1]), acts.dtype)

        def turn(r, c):
            turned[:, tile(r)] = rows[r, :ROWBLK, :feat].T
            return c

        lax.fori_loop(0, t.rows, turn, 0)

    for ref in (grad_gate, grad_up, grad_down):
        ref[...] = jnp.zeros_like(ref)

    def block(i, c):
        b = step * together + i

        def two(j, c):
            live = t.rows * b + 2 * j
            picked = [table[t.live_row + live], table[t.live_row + live + 1]]
            act = jnp.concatenate([acts[tile(listed(t, units, table[t.live_at + live + k])), :] for k in (0, 1)], axis=0)
            both = nn(jnp.concatenate([turned[:, tile(r)] for r in picked], axis=1), act[:, BLK:]) * scale
            cot = jnp.concatenate([rows[r, :ROWBLK, feat:] for r in picked], axis=0)
            grad_gate[:, tile(i)] += both[:, :BLK]
            grad_up[:, tile(i)] += both[:, BLK:]
            grad_down[tile(i), :] += nn(act[:, :BLK].T, cot) * scale
            return c

        return lax.fori_loop(0, (table[t.live + b] + 1) // 2, two, c)

    lax.fori_loop(0, together, block, 0)


def copies(array, axis):
    n = lax.axis_size(axis)
    return lax.all_to_all(jnp.broadcast_to(array[None], (n, *array.shape)), axis, 0, 0, tiled=True)


def across(array):
    return lax.ppermute(array, "core", [(0, 1), (1, 0)])


def onward(array, d):
    n = lax.axis_size("x")
    return lax.ppermute(array, "x", [(i, (i + d) % n) for i in range(n)])


def summed(array, axis):
    n = lax.axis_size(axis)
    tiles = array.reshape(n, array.shape[0] // n, array.shape[1])
    return lax.all_to_all(tiles, axis, 0, 0, tiled=True).astype(F32).sum(axis=0)


def summed_scaled(array, axis):
    n = lax.axis_size(axis)
    size, columns = array.shape[0] // n, array.shape[1]
    peak = jnp.max(jnp.abs(array), axis=0, keepdims=True)
    power = jnp.round(jnp.clip(jnp.log2(jnp.maximum(peak, 1e-36)), -119.0, 119.0))
    tiles = (array * jnp.exp2(-power)).astype(jnp.float16).reshape(n, size, columns)
    powers = jnp.broadcast_to(power.astype(jnp.float16), (n, 16, columns))
    arrived = lax.all_to_all(jnp.concatenate([tiles, powers], axis=1), axis, 0, 0, tiled=True).astype(F32)
    return jnp.sum(arrived[:, :size] * jnp.exp2(arrived[:, size : size + 1]), axis=0)


def activations(parts):
    sums = summed_scaled(summed(parts, "x"), "zh")
    gate, up, grad = sums[:, :BLK], sums[:, BLK : 2 * BLK], sums[:, 2 * BLK :]
    s = jax.nn.sigmoid(gate)
    acts = jnp.concatenate(
        [
            (jax.nn.silu(gate) * up).astype(BF16),
            (grad * up * s * (1.0 + gate * (1.0 - s))).astype(BF16),
            (grad * gate * s).astype(BF16),
        ],
        axis=1,
    )
    own = copies(acts, "zh").reshape(-1, 3 * BLK)
    half = own.shape[0] // 2
    before, after = onward(own, 1), onward(own, -1)
    far = jnp.concatenate([onward(before[:half], 1), onward(after[half:], -1)], axis=0)
    blocks = own, jnp.concatenate([before, after], axis=0), far
    return *blocks, *map(across, blocks)


def from_rows(units, place, table, rows, rows_other, gate, gate_other, up, up_other, down, down_other, t):
    feat = down.shape[1]
    parts = pl.pallas_call(
        functools.partial(partials_kernel, t, units, feat),
        out_shape=jax.ShapeDtypeStruct(((BASE * t.rows + EXTRA * units) // 2 * ROWBLK, 3 * BLK), BF16),
        in_specs=[SMEM, SMEM] + [VMEM] * 8,
        out_specs=VMEM,
        compiler_params=PARAMS,
        name="partials",
    )(place, table, rows, rows_other, gate, gate_other, up, up_other, down, down_other)
    acts = activations(parts)

    scratch = [pltpu.VMEM(((t.pairs + 1) * BLK, 3 * BLK), BF16)]
    partial_rows = pl.pallas_call(
        functools.partial(rows_kernel, t, units),
        out_shape=jax.ShapeDtypeStruct((t.rows * ROWBLK, 2 * feat), BF16),
        in_specs=[SMEM, SMEM] + [ANY] * 6 + [VMEM] * 3,
        out_specs=pl.BlockSpec(memory_space=pltpu.HBM),
        scratch_shapes=scratch
        + [
            pltpu.VMEM((ROWBLK, 2 * feat), F32),
            pltpu.VMEM((t.rows * ROWBLK, 2 * feat), BF16),
            pltpu.SemaphoreType.DMA((9,)),
        ],
        compiler_params=PARAMS,
        name="row_grads",
    )(place, table, *acts, gate, up, down)
    out_rows = summed(partial_rows, TP).astype(BF16)

    together = 2 if t.blocks % 2 == 0 else 1
    columns = pl.BlockSpec((feat, together * BLK), lambda b: (0, b))
    grad_gate, grad_up, grad_down = pl.pallas_call(
        functools.partial(weights_kernel, t, units, together, (t.rows * ROWBLK) ** -0.5),
        grid=(t.blocks // together,),
        out_shape=(
            jax.ShapeDtypeStruct(gate.shape, F32),
            jax.ShapeDtypeStruct(up.shape, F32),
            jax.ShapeDtypeStruct(down.shape, F32),
        ),
        in_specs=[SMEM, SMEM] + [ANY] * 6 + [VMEM],
        out_specs=(columns, columns, pl.BlockSpec((together * BLK, feat), lambda b: (b, 0))),
        scratch_shapes=scratch + [pltpu.VMEM((feat, t.rows * ROWBLK), BF16), pltpu.SemaphoreType.DMA((8,))],
        compiler_params=PARAMS,
        name="weight_grads",
    )(place, table, *acts, rows)
    return out_rows[:, :feat], out_rows[:, feat:], grad_gate, grad_up, grad_down


def shards(tokens, gate, up, down, masks, cotangent):
    own_rows, feat = tokens.shape
    t = Table(*masks.shape)
    place = jnp.stack([lax.axis_index("core"), lax.axis_index("x")]).astype(jnp.int32)
    payload = pl.pallas_call(
        functools.partial(payload_kernel, BASE),
        out_shape=jax.ShapeDtypeStruct((lax.axis_size(TP), own_rows + 16, 2 * feat), BF16),
        in_specs=[SMEM, VMEM, VMEM],
        out_specs=VMEM,
        name="payload",
    )(masks, tokens, cotangent)
    table = pl.pallas_call(
        functools.partial(table_kernel, t),
        out_shape=jax.ShapeDtypeStruct((t.size,), jnp.int32),
        in_specs=[SMEM],
        out_specs=SMEM,
        name="pair_table",
    )(masks)
    gate_other, up_other, down_other = across(gate), across(up), across(down)
    rows = lax.all_to_all(payload, TP, 0, 0, tiled=True)
    rows, table, gate_other, up_other, down_other = lax.optimization_barrier(
        (rows, table, gate_other, up_other, down_other)
    )
    rows_other = across(rows)
    most = jnp.max(rows[:, own_rows, 0].astype(F32))
    path = sum((most > room).astype(jnp.int32) for room in ROOM[:-1])
    paths = [functools.partial(from_rows, units, t=t) for units in ROOM]
    return lax.switch(
        path, paths, place, table, rows, rows_other, gate, gate_other, up, up_other, down, down_other
    )


def solution(mesh):
    fine = Mesh(mesh.devices.reshape(4, 4, 2, 2, 4), SEQ + TP)
    wide, tall = P(SEQ, TP), P(TP, SEQ)
    return jax.shard_map(
        shards,
        mesh=fine,
        in_specs=(tall, wide, wide, tall, P(None, TP), tall),
        out_specs=(tall, tall, wide, wide, tall),
        check_vma=False,
    )
```

profile of v0, /device:TPU:1, one launch (start us, length us, event | category | flops | bytes accessed | tf_op | source)
XLA Modules:
  0.0 150.4 jit_solution(17079746132418377269)
XLA Ops:
  0.6 0.0 copy-start.10
  0.6 0.0 copy-start.17
  0.7 2.1 %payload.1 = bf16[8,144,512]{2,1,0:T(8,128)(2,1)} custom-call(s32[8,14]{1,0:T(8,128)} %masks.3, bf16[128,256]{1,0:T(8,128)(2,1)} %tokens.1, bf16[128,256]{1,0:T(8,128)(2,1)} %cotangent.1), custom_call_target="tpu_custom_call" | custom-call | tf_op jit(solution)/shard_map/payload/pallas_call | solution.py:324
  2.8 6.4 %all-to-all-start.12 = ((bf16[8,144,512]{2,1,0:T(8,128)(2,1)}), bf16[8,144,512]{2,1,0:T(8,128)(2,1)S(1)}, u32[]{:S(2)}, u32[]{:S(2)}) async-start(bf16[8,144,512]{2,1,0:T(8,128)(2,1)} %payload.1), calls=%async_computation.12 | async-start | bytes 2359296 | tf_op jit(solution)/shard_map/all_to_all | solution.py:339
  9.1 0.0 copy-done.10
  9.1 1.0 collective-permute-start.21
  10.2 0.0 copy-done.17
  10.2 0.1 collective-permute-start.22
  10.3 0.4 collective-permute-start.23
  10.7 2.2 %pair_table.1 = s32[311]{0:T(512)S(1)} custom-call(s32[8,14]{1,0:T(8,128)} %masks.3), custom_call_target="tpu_custom_call" | custom-call | tf_op jit(solution)/shard_map/pair_table/pallas_call | solution.py:331
  13.0 0.0 collective-permute-done.21
  13.0 2.1 %collective-permute-done.22 = bf16[256,1792]{1,0:T(8,128)(2,1)} collective-permute-done((bf16[256,1792]{1,0:T(8,128)(2,1)S(1)}, bf16[256,1792]{1,0:T(8,128)(2,1)}, u32[]{:S(2)}, u32[]{:S(2)}) %collective-permute-start.22) | collective-permute-done | bytes 917536 | tf_op jit(solution)/shard_map/ppermute | solution.py:227
  15.0 0.2 collective-permute-done.23
  15.3 10.2 %all-to-all-done.12 = bf16[8,144,512]{2,1,0:T(8,128)(2,1)S(1)} async-done(((bf16[8,144,512]{2,1,0:T(8,128)(2,1)}), bf16[8,144,512]{2,1,0:T(8,128)(2,1)S(1)}, u32[]{:S(2)}, u32[]{:S(2)}) %all-to-all-start.12) | async-done | bytes 1179680 | tf_op jit(solution)/shard_map/all_to_all | solution.py:339
  25.5 0.8 collective-permute-start.24
  26.3 0.1 pad_add_fusion
  26.4 0.6 slice_reduce_fusion
  28.3 0.6 collective-permute-done.24
  28.9 120.8 %conditional.1 = (f32[256,1792]{1,0:T(8,128)}, f32[256,1792]{1,0:T(8,128)}, f32[1792,256]{1,0:T(8,128)}, bf16[128,256]{1,0:T(8,128)(2,1)S(1)}, bf16[128,256]{1,0:T(8,128)(2,1)S(1)}) conditional(s32[]{:T(128)} %clamp.27, (s32[2]{0:T(128)S(1)}, s32[311]{0:T(512)S(1)}, bf16[8,144,512]{2,1,0:T(8,128)(2,1)S(1)}, ...), branch_computations={%region_1.6_spmd, %region_6.11_spmd, %region_11.16_spmd} | conditional | flops 6561536 | bytes 96278752 | solution.py:347
  28.9 0.0 copy-start.8
  28.9 4.9 %partials.4 = bf16[2304,384]{1,0:T(8,128)(2,1)S(1)} custom-call(s32[2]{0:T(128)S(1)} %get-tuple-element.73.place, s32[311]{0:T(512)S(1)} %get-tuple-element.74.table, bf16[8,144,512]{2,1,0:T(8,128)(2,1)S(1)} %get-tuple-element.75.own.refs_6_, bf16[8,144,512]{2,1,0:T(8,128)(2,1)} %get-tuple-element.76.other, ...), custom_call_target="tpu_custom_call" | custom-call | tf_op jit(solution)/shard_map/cond/branch_1_fun/partials/pallas_call | solution.py:274
  33.8 0.0 copy-done.8
  33.9 0.0 copy-done.13
  33.9 0.0 copy-done.20
  33.9 26.1 %all_to_all.56 = bf16[4,576,384]{2,1,0:T(8,128)(2,1)S(1)} all-to-all(bf16[4,576,384]{2,1,0:T(8,128)(2,1)S(1)} %bitcast.24), channel_id=1, replica_groups=mesh['x'=4,'zh'=4,'core'=2,'zl'=2,'y'=4] {'x'}, dimensions={0} | all-to-all | bytes 3538944 | tf_op jit(solution)/shard_map/cond/branch_1_fun/all_to_all | solution.py:238
  59.9 0.2 convert_reduce_fusion.1
  60.2 0.1 abs_reduce_fusion.1
  60.3 0.1 multiply_convert_fusion.4
  60.4 0.1 pad_maximum_fusion.2
  60.5 18.3 %all_to_all.57 = f16[4,160,384]{2,1,0:T(8,128)(2,1)S(1)} all-to-all(f16[4,160,384]{2,1,0:T(8,128)(2,1)S(1)} %pad_maximum_fusion.2), channel_id=1, replica_groups=mesh['x'=4,'zh'=4,'core'=2,'zl'=2,'y'=4] {'zh'}, dimensions={0} | all-to-all | bytes 983040 | tf_op jit(solution)/shard_map/cond/branch_1_fun/all_to_all | solution.py:248
  78.8 0.1 convert_element_type.75
  78.9 0.1 fusion.3
  78.9 0.1 multiply_convert_fusion.7
  79.1 15.1 %all_to_all.58 = bf16[4,144,384]{2,1,0:T(8,128)(2,1)S(1)} all-to-all(bf16[4,144,384]{2,1,0:T(8,128)(2,1)S(1)} %broadcast_in_dim.17), channel_id=1, replica_groups=mesh['x'=4,'zh'=4,'core'=2,'zl'=2,'y'=4] {'zh'}, dimensions={0} | all-to-all | bytes 884736 | tf_op jit(solution)/shard_map/cond/branch_1_fun/all_to_all | solution.py:223
  94.1 0.3 collective-permute-start.7
  94.4 2.4 %collective-permute-start.8 = (bf16[576,384]{1,0:T(8,128)(2,1)S(1)}, bf16[576,384]{1,0:T(8,128)(2,1)S(1)}, u32[]{:S(2)}, u32[]{:S(2)}) collective-permute-start(bf16[576,384]{1,0:T(8,128)(2,1)S(1)} %bitcast.33), channel_id=1, source_target_pairs={{0,192},{64,0},{128,64},{192,128},{1,193},{65,1},{129,65},{193,129... | collective-permute-start | bytes 1327112 | tf_op jit(solution)/shard_map/cond/branch_1_fun/ppermute | solution.py:232
  96.8 5.7 %collective-permute-done.7 = bf16[576,384]{1,0:T(8,128)(2,1)S(1)} collective-permute-done((bf16[576,384]{1,0:T(8,128)(2,1)S(1)}, bf16[576,384]{1,0:T(8,128)(2,1)S(1)}, u32[]{:S(2)}, u32[]{:S(2)}) %collective-permute-start.7) | collective-permute-done | bytes 442400 | tf_op jit(solution)/shard_map/cond/branch_1_fun/ppermute | solution.py:232
  102.5 0.0 copy-start.14
  102.5 0.0 copy-start.21
  102.5 0.0 copy-start.25
  102.5 0.1 collective-permute-start.9
  102.7 0.0 collective-permute-done.8
  102.7 0.1 constant_dynamic-update-slice_fusion.4.refs_1_
  102.8 9.7 %collective-permute-start.12 = (bf16[1152,384]{1,0:T(8,128)(2,1)S(1)}, bf16[1152,384]{1,0:T(8,128)(2,1)S(1)}, u32[]{:S(2)}, u32[]{:S(2)}) collective-permute-start(bf16[1152,384]{1,0:T(8,128)(2,1)S(1)} %constant_dynamic-update-slice_fusion.4.refs_1_), channel_id=1, source_target_pairs={{0,8},{8,0},{1,9},{9,1},{2,10},{10,2},{3,11},{11,3},{4,12},{12,4},... | collective-permute-start | bytes 2654216 | tf_op jit(solution)/shard_map/cond/branch_1_fun/ppermute | solution.py:227
  112.6 3.0 %collective-permute-start.10 = (bf16[288,384]{1,0:T(8,128)(2,1)S(1)}, bf16[288,384]{1,0:T(8,128)(2,1)S(1)}, u32[]{:S(2)}, u32[]{:S(2)}) collective-permute-start(bf16[288,384]{1,0:T(8,128)(2,1)S(1)} %slice.100), channel_id=1, source_target_pairs={{0,192},{64,0},{128,64},{192,128},{1,193},{65,1},{129,65},{193,129... | collective-permute-start | bytes 663560 | tf_op jit(solution)/shard_map/cond/branch_1_fun/ppermute | solution.py:232
  115.6 0.3 collective-permute-start.11
  115.9 0.0 collective-permute-done.9
  115.9 4.5 %collective-permute-done.10 = bf16[288,384]{1,0:T(8,128)(2,1)S(1)} collective-permute-done((bf16[288,384]{1,0:T(8,128)(2,1)S(1)}, bf16[288,384]{1,0:T(8,128)(2,1)S(1)}, u32[]{:S(2)}, u32[]{:S(2)}) %collective-permute-start.10) | collective-permute-done | bytes 221216 | tf_op jit(solution)/shard_map/cond/branch_1_fun/ppermute | solution.py:232
  120.4 0.9 collective-permute-start.13
  121.3 0.0 collective-permute-done.11.refs_3_
  121.3 1.4 collective-permute-done.13.refs_5_
  122.8 0.0 collective-permute-done.12.refs_4_
  122.8 0.0 copy-done.14
  122.8 0.0 copy-done.21
  122.8 0.0 copy-done.25
  122.8 6.0 %row_grads.4 = bf16[1024,512]{1,0:T(8,128)(2,1)} custom-call(s32[2]{0:T(128)S(1)} %get-tuple-element.73.place, s32[311]{0:T(512)S(1)} %get-tuple-element.74.table, bf16[576,384]{1,0:T(8,128)(2,1)S(1)} %bitcast.35, bf16[1152,384]{1,0:T(8,128)(2,1)S(1)} %constant_dynamic-update-slice_fusion.4.refs_1_, ...), custom_call_target="tpu_custom_call" | custom-call | tf_op jit(solution)/shard_map/cond/branch_1_fun/row_grads/pallas_call | solution.py:285
  128.8 4.3 %all-to-all-start.7 = ((bf16[8,128,512]{2,1,0:T(8,128)(2,1)}), bf16[8,128,512]{2,1,0:T(8,128)(2,1)}, u32[]{:S(2)}, u32[]{:S(2)}) async-start(bf16[8,128,512]{2,1,0:T(8,128)(2,1)} %bitcast.7), calls=%async_computation.7 | async-start | bytes 2097152 | tf_op jit(solution)/shard_map/cond/branch_1_fun/all_to_all | solution.py:238
  133.0 10.5 %weight_grads.4 = (f32[256,1792]{1,0:T(8,128)}, f32[256,1792]{1,0:T(8,128)}, f32[1792,256]{1,0:T(8,128)}) custom-call(s32[2]{0:T(128)S(1)} %get-tuple-element.73.place, s32[311]{0:T(512)S(1)} %get-tuple-element.74.table, bf16[576,384]{1,0:T(8,128)(2,1)S(1)} %bitcast.36, bf16[1152,384]{1,0:T(8,128)(2,1)S(1)} %constant_dynamic-update-slice_fusion.4.refs_1_, ...), custom_call_target="tpu_custom_call" | custom-call | tf_op jit(solution)/shard_map/cond/branch_1_fun/weight_grads/pallas_call | solution.py:303
  143.6 4.5 %all-to-all-done.7 = bf16[8,128,512]{2,1,0:T(8,128)(2,1)} async-done(((bf16[8,128,512]{2,1,0:T(8,128)(2,1)}), bf16[8,128,512]{2,1,0:T(8,128)(2,1)}, u32[]{:S(2)}, u32[]{:S(2)}) %all-to-all-start.7) | async-done | bytes 1048608 | tf_op jit(solution)/shard_map/cond/branch_1_fun/all_to_all | solution.py:238
  148.0 1.4 reduce_sum.91
  149.7 0.0 copy-start.27
  149.7 0.0 copy-start.28
  149.7 0.6 copy-done.27
  150.3 0.0 copy-done.28
  (14 shorter events, 0.3 us)
Async XLA Ops:
  0.6 8.5 %copy-start.10 = (bf16[256,1792]{1,0:T(8,128)(2,1)S(1)}, bf16[256,1792]{1,0:T(8,128)(2,1)}, u32[]{:S(2)}) copy-start(bf16[256,1792]{1,0:T(8,128)(2,1)} %param.10) | copy-start | bytes 2752516
  0.6 9.6 %copy-start.17 = (bf16[256,1792]{1,0:T(8,128)(2,1)S(1)}, bf16[256,1792]{1,0:T(8,128)(2,1)}, u32[]{:S(2)}) copy-start(bf16[256,1792]{1,0:T(8,128)(2,1)} %param.11) | copy-start | bytes 2752516
  2.8 22.7 %all-to-all-start.12 = ((bf16[8,144,512]{2,1,0:T(8,128)(2,1)}), bf16[8,144,512]{2,1,0:T(8,128)(2,1)S(1)}, u32[]{:S(2)}, u32[]{:S(2)}) async-start(bf16[8,144,512]{2,1,0:T(8,128)(2,1)} %payload.1), calls=%async_computation.12 | async-start | bytes 2359296 | tf_op jit(solution)/shard_map/all_to_all | solution.py:339
  9.1 3.8 %collective-permute-start.21 = (bf16[256,1792]{1,0:T(8,128)(2,1)S(1)}, bf16[256,1792]{1,0:T(8,128)(2,1)}, u32[]{:S(2)}, u32[]{:S(2)}) collective-permute-start(bf16[256,1792]{1,0:T(8,128)(2,1)S(1)} %copy-done.10), channel_id=1, source_target_pairs={{0,8},{8,0},{1,9},{9,1},{2,10},{10,2},{3,11},{11,3},{4,12},{12,4},... | collective-permute-start | bytes 2752520 | tf_op jit(solution)/shard_map/ppermute | solution.py:227
  10.2 4.9 %collective-permute-start.22 = (bf16[256,1792]{1,0:T(8,128)(2,1)S(1)}, bf16[256,1792]{1,0:T(8,128)(2,1)}, u32[]{:S(2)}, u32[]{:S(2)}) collective-permute-start(bf16[256,1792]{1,0:T(8,128)(2,1)S(1)} %copy-done.17), channel_id=1, source_target_pairs={{0,8},{8,0},{1,9},{9,1},{2,10},{10,2},{3,11},{11,3},{4,12},{12,4},... | collective-permute-start | bytes 2752520 | tf_op jit(solution)/shard_map/ppermute | solution.py:227
  10.3 5.0 %collective-permute-start.23 = (bf16[1792,256]{1,0:T(8,128)(2,1)}, bf16[1792,256]{1,0:T(8,128)(2,1)}, u32[]{:S(2)}, u32[]{:S(2)}) collective-permute-start(bf16[1792,256]{1,0:T(8,128)(2,1)} %param.12), channel_id=1, source_target_pairs={{0,8},{8,0},{1,9},{9,1},{2,10},{10,2},{3,11},{11,3},{4,12},{12,4},... | collective-permute-start | bytes 2752520 | tf_op jit(solution)/shard_map/ppermute | solution.py:227
  25.5 3.5 %collective-permute-start.24 = (bf16[8,144,512]{2,1,0:T(8,128)(2,1)S(1)}, bf16[8,144,512]{2,1,0:T(8,128)(2,1)}, u32[]{:S(2)}, u32[]{:S(2)}) collective-permute-start(bf16[8,144,512]{2,1,0:T(8,128)(2,1)S(1)} %all-to-all-done.12), channel_id=1, source_target_pairs={{0,8},{8,0},{1,9},{9,1},{2,10},{10,2},{3,11},{11,3},{4,12},{12,4},... | collective-permute-start | bytes 3538952 | tf_op jit(solution)/shard_map/ppermute | solution.py:227
  28.9 4.9 %copy-start.8 = (bf16[8,144,512]{2,1,0:T(8,128)(2,1)}, bf16[8,144,512]{2,1,0:T(8,128)(2,1)S(1)}, u32[]{:S(2)}) copy-start(bf16[8,144,512]{2,1,0:T(8,128)(2,1)S(1)} %get-tuple-element.75.own.refs_6_) | copy-start | bytes 3538948 | tf_op jit(solution)/shard_map/cond
  28.9 4.9 %copy-start.13 = (bf16[256,1792]{1,0:T(8,128)(2,1)}, bf16[256,1792]{1,0:T(8,128)(2,1)S(1)}, u32[]{:S(2)}) copy-start(bf16[256,1792]{1,0:T(8,128)(2,1)S(1)} %get-tuple-element.77.gate_own.refs_6_) | copy-start | bytes 2752516 | tf_op jit(solution)/shard_map/cond
  28.9 5.0 %copy-start.20 = (bf16[256,1792]{1,0:T(8,128)(2,1)}, bf16[256,1792]{1,0:T(8,128)(2,1)S(1)}, u32[]{:S(2)}) copy-start(bf16[256,1792]{1,0:T(8,128)(2,1)S(1)} %get-tuple-element.79.up_own.refs_7_) | copy-start | bytes 2752516 | tf_op jit(solution)/shard_map/cond
  94.1 8.4 %collective-permute-start.7 = (bf16[576,384]{1,0:T(8,128)(2,1)S(1)}, bf16[576,384]{1,0:T(8,128)(2,1)S(1)}, u32[]{:S(2)}, u32[]{:S(2)}) collective-permute-start(bf16[576,384]{1,0:T(8,128)(2,1)S(1)} %bitcast.32), channel_id=1, source_target_pairs={{0,64},{64,128},{128,192},{192,0},{1,65},{65,129},{129,193},{193,1... | collective-permute-start | bytes 1327112 | tf_op jit(solution)/shard_map/cond/branch_1_fun/ppermute | solution.py:232
  94.4 8.3 %collective-permute-start.8 = (bf16[576,384]{1,0:T(8,128)(2,1)S(1)}, bf16[576,384]{1,0:T(8,128)(2,1)S(1)}, u32[]{:S(2)}, u32[]{:S(2)}) collective-permute-start(bf16[576,384]{1,0:T(8,128)(2,1)S(1)} %bitcast.33), channel_id=1, source_target_pairs={{0,192},{64,0},{128,64},{192,128},{1,193},{65,1},{129,65},{193,129... | collective-permute-start | bytes 1327112 | tf_op jit(solution)/shard_map/cond/branch_1_fun/ppermute | solution.py:232
  102.5 20.2 %copy-start.14 = (bf16[256,1792]{1,0:T(8,128)(2,1)S(1)}, bf16[256,1792]{1,0:T(8,128)(2,1)}, u32[]{:S(2)}) copy-start(bf16[256,1792]{1,0:T(8,128)(2,1)} %copy-done.13) | copy-start | bytes 2752516 | tf_op jit(solution)/shard_map/cond
  102.5 20.2 %copy-start.21 = (bf16[256,1792]{1,0:T(8,128)(2,1)S(1)}, bf16[256,1792]{1,0:T(8,128)(2,1)}, u32[]{:S(2)}) copy-start(bf16[256,1792]{1,0:T(8,128)(2,1)} %copy-done.20) | copy-start | bytes 2752516 | tf_op jit(solution)/shard_map/cond
  102.5 20.2 %copy-start.25 = (bf16[1792,256]{1,0:T(8,128)(2,1)S(1)}, bf16[1792,256]{1,0:T(8,128)(2,1)}, u32[]{:S(2)}) copy-start(bf16[1792,256]{1,0:T(8,128)(2,1)} %get-tuple-element.81.down_own.refs_8_) | copy-start | bytes 2752516 | tf_op jit(solution)/shard_map/cond
  102.5 13.3 %collective-permute-start.9 = (bf16[288,384]{1,0:T(8,128)(2,1)S(1)}, bf16[288,384]{1,0:T(8,128)(2,1)S(1)}, u32[]{:S(2)}, u32[]{:S(2)}) collective-permute-start(bf16[288,384]{1,0:T(8,128)(2,1)S(1)} %slice.99), channel_id=1, source_target_pairs={{0,64},{64,128},{128,192},{192,0},{1,65},{65,129},{129,193},{193,1... | collective-permute-start | bytes 663560 | tf_op jit(solution)/shard_map/cond/branch_1_fun/ppermute | solution.py:232
  102.8 20.0 %collective-permute-start.12 = (bf16[1152,384]{1,0:T(8,128)(2,1)S(1)}, bf16[1152,384]{1,0:T(8,128)(2,1)S(1)}, u32[]{:S(2)}, u32[]{:S(2)}) collective-permute-start(bf16[1152,384]{1,0:T(8,128)(2,1)S(1)} %constant_dynamic-update-slice_fusion.4.refs_1_), channel_id=1, source_target_pairs={{0,8},{8,0},{1,9},{9,1},{2,10},{10,2},{3,11},{11,3},{4,12},{12,4},... | collective-permute-start | bytes 2654216 | tf_op jit(solution)/shard_map/cond/branch_1_fun/ppermute | solution.py:227
  112.6 7.9 %collective-permute-start.10 = (bf16[288,384]{1,0:T(8,128)(2,1)S(1)}, bf16[288,384]{1,0:T(8,128)(2,1)S(1)}, u32[]{:S(2)}, u32[]{:S(2)}) collective-permute-start(bf16[288,384]{1,0:T(8,128)(2,1)S(1)} %slice.100), channel_id=1, source_target_pairs={{0,192},{64,0},{128,64},{192,128},{1,193},{65,1},{129,65},{193,129... | collective-permute-start | bytes 663560 | tf_op jit(solution)/shard_map/cond/branch_1_fun/ppermute | solution.py:232
  115.6 5.8 %collective-permute-start.11 = (bf16[576,384]{1,0:T(8,128)(2,1)S(1)}, bf16[576,384]{1,0:T(8,128)(2,1)S(1)}, u32[]{:S(2)}, u32[]{:S(2)}) collective-permute-start(bf16[576,384]{1,0:T(8,128)(2,1)S(1)} %bitcast.34), channel_id=1, source_target_pairs={{0,8},{8,0},{1,9},{9,1},{2,10},{10,2},{3,11},{11,3},{4,12},{12,4},... | collective-permute-start | bytes 1327112 | tf_op jit(solution)/shard_map/cond/branch_1_fun/ppermute | solution.py:227
  120.4 2.3 %collective-permute-start.13 = (bf16[576,384]{1,0:T(8,128)(2,1)S(1)}, bf16[576,384]{1,0:T(8,128)(2,1)S(1)}, u32[]{:S(2)}, u32[]{:S(2)}) collective-permute-start(bf16[576,384]{1,0:T(8,128)(2,1)S(1)} %constant_dynamic-update-slice_fusion.6.refs_2_), channel_id=1, source_target_pairs={{0,8},{8,0},{1,9},{9,1},{2,10},{10,2},{3,11},{11,3},{4,12},{12,4},... | collective-permute-start | bytes 1327112 | tf_op jit(solution)/shard_map/cond/branch_1_fun/ppermute | solution.py:227
  128.8 19.3 %all-to-all-start.7 = ((bf16[8,128,512]{2,1,0:T(8,128)(2,1)}), bf16[8,128,512]{2,1,0:T(8,128)(2,1)}, u32[]{:S(2)}, u32[]{:S(2)}) async-start(bf16[8,128,512]{2,1,0:T(8,128)(2,1)} %bitcast.7), calls=%async_computation.7 | async-start | bytes 2097152 | tf_op jit(solution)/shard_map/cond/branch_1_fun/all_to_all | solution.py:238
  149.7 0.6 copy-start.27
  149.7 0.6 copy-start.28
where the time goes:
time: 148 us; the launch traced here: 150 us
  blocking collectives  59.4 us (40%)
  starting transfers between devices  29.7 us (20%)
  waiting for transfers between devices  29.2 us (20%)
  Pallas kernels  25.8 us (17%)
  other arithmetic  2.8 us (2%)
  between operations  2.01 us (1%)
    all_to_all x1, blocking collectives, summed(): return lax.all_to_all(tiles, axis, 0, 0, tiled=True).astype(F32).sum(axis=0)  26.1 us
    all_to_all x1, blocking collectives, summed_scaled(): lax.all_to_all(jnp.concatenate([tiles, powers], axis=1), axis, 0, 0, tile...  18.3 us
    all_to_all x1, blocking collectives, copies(): lax.all_to_all(jnp.broadcast_to(array[None], (n, *array.shape)), axis, 0,...  15.1 us
    ppermute x7, starting transfers between devices, across(): return lax.ppermute(array, 'core', [(0, 1), (1, 0)])  13.3 us
    pallas_call x1, Pallas kernels, from_rows(): pl.pallas_call(functools.partial(weights_kernel, t, units, together, (t.r...  10.5 us
    ppermute x4, waiting for transfers between devices, onward(): return lax.ppermute(array, 'x', [(i, (i + d) % n) for i in range(n)])  10.2 us
    all_to_all x1, waiting for transfers between devices, shards(): rows = lax.all_to_all(payload, TP, 0, 0, tiled=True)  10.2 us
    all_to_all x1, starting transfers between devices, shards(): rows = lax.all_to_all(payload, TP, 0, 0, tiled=True)  6.37 us
  transfers between devices with their start and end apart: 13, of which 8 were waited for; matrix products, arithmetic and copies ran while one was open for 1% of the time, Pallas kernels for 8%

commit v1 on v0

--- a/solution.py
+++ b/solution.py
@@ -176,7 +176,7 @@
         pltpu.make_async_copy(done.at[tile(r)], out.at[tile(r)], sems.at[8]).start()
         return c
 
-    lax.fori_loop(0, t.rows, row, 0, unroll=2 if units < t.rows else 1)
+    lax.fori_loop(0, t.rows, row, 0)
     pltpu.make_async_copy(done, out, sems.at[8]).wait()
 
 

time: 148 us -> 152 us (1.027); the launches traced: 150 us -> 151 us
  no operation moved by 1% of the time
where the time goes in v1:
time: 152 us; the launch traced here: 151 us
  blocking collectives  59 us (39%)
  starting transfers between devices  30 us (20%)
  waiting for transfers between devices  29.6 us (19%)
  Pallas kernels  25.4 us (17%)
  other arithmetic  2.8 us (2%)
  between operations  2.01 us (1%)
    all_to_all x1, blocking collectives, summed(): return lax.all_to_all(tiles, axis, 0, 0, tiled=True).astype(F32).sum(axis=0)  26 us
    all_to_all x1, blocking collectives, summed_scaled(): lax.all_to_all(jnp.concatenate([tiles, powers], axis=1), axis, 0, 0, tile...  18.1 us
    all_to_all x1, blocking collectives, copies(): lax.all_to_all(jnp.broadcast_to(array[None], (n, *array.shape)), axis, 0,...  14.8 us
    ppermute x7, starting transfers between devices, across(): return lax.ppermute(array, 'core', [(0, 1), (1, 0)])  13.6 us
    ppermute x4, waiting for transfers between devices, onward(): return lax.ppermute(array, 'x', [(i, (i + d) % n) for i in range(n)])  10.2 us
    all_to_all x1, waiting for transfers between devices, shards(): rows = lax.all_to_all(payload, TP, 0, 0, tiled=True)  10.2 us
    pallas_call x1, Pallas kernels, from_rows(): pl.pallas_call(functools.partial(weights_kernel, t, units, together, (t.r...  10.1 us
    all_to_all x1, starting transfers between devices, shards(): rows = lax.all_to_all(payload, TP, 0, 0, tiled=True)  6.37 us
  transfers between devices with their start and end apart: 13, of which 8 were waited for; matrix products, arithmetic and copies ran while one was open for 1% of the time, Pallas kernels for 8%

profile of v1, /device:TPU:1, one launch (start us, length us, event | category | flops | bytes accessed | tf_op | source)
XLA Modules:
  0.0 150.5 jit_solution(12195724359933039585)
XLA Ops:
  0.6 0.0 copy-start.10
  0.6 0.0 copy-start.17
  0.7 2.1 %payload.1 = bf16[8,144,512]{2,1,0:T(8,128)(2,1)} custom-call(s32[8,14]{1,0:T(8,128)} %masks.3, bf16[128,256]{1,0:T(8,128)(2,1)} %tokens.1, bf16[128,256]{1,0:T(8,128)(2,1)} %cotangent.1), custom_call_target="tpu_custom_call" | custom-call | tf_op jit(solution)/shard_map/payload/pallas_call | solution.py:324
  2.8 6.4 %all-to-all-start.12 = ((bf16[8,144,512]{2,1,0:T(8,128)(2,1)}), bf16[8,144,512]{2,1,0:T(8,128)(2,1)S(1)}, u32[]{:S(2)}, u32[]{:S(2)}) async-start(bf16[8,144,512]{2,1,0:T(8,128)(2,1)} %payload.1), calls=%async_computation.12 | async-start | bytes 2359296 | tf_op jit(solution)/shard_map/all_to_all | solution.py:339
  9.1 0.0 copy-done.10
  9.1 1.0 collective-permute-start.21
  10.2 0.0 copy-done.17
  10.2 0.1 collective-permute-start.22
  10.3 0.4 collective-permute-start.23
  10.7 2.2 %pair_table.1 = s32[311]{0:T(512)S(1)} custom-call(s32[8,14]{1,0:T(8,128)} %masks.3), custom_call_target="tpu_custom_call" | custom-call | tf_op jit(solution)/shard_map/pair_table/pallas_call | solution.py:331
  13.0 0.0 collective-permute-done.21
  13.0 2.1 %collective-permute-done.22 = bf16[256,1792]{1,0:T(8,128)(2,1)} collective-permute-done((bf16[256,1792]{1,0:T(8,128)(2,1)S(1)}, bf16[256,1792]{1,0:T(8,128)(2,1)}, u32[]{:S(2)}, u32[]{:S(2)}) %collective-permute-start.22) | collective-permute-done | bytes 917536 | tf_op jit(solution)/shard_map/ppermute | solution.py:227
  15.0 0.2 collective-permute-done.23
  15.3 10.2 %all-to-all-done.12 = bf16[8,144,512]{2,1,0:T(8,128)(2,1)S(1)} async-done(((bf16[8,144,512]{2,1,0:T(8,128)(2,1)}), bf16[8,144,512]{2,1,0:T(8,128)(2,1)S(1)}, u32[]{:S(2)}, u32[]{:S(2)}) %all-to-all-start.12) | async-done | bytes 1179680 | tf_op jit(solution)/shard_map/all_to_all | solution.py:339
  25.5 0.8 collective-permute-start.24
  26.3 0.1 pad_add_fusion
  26.4 0.6 slice_reduce_fusion
  28.3 0.6 collective-permute-done.24
  28.9 120.9 %conditional.1 = (f32[256,1792]{1,0:T(8,128)}, f32[256,1792]{1,0:T(8,128)}, f32[1792,256]{1,0:T(8,128)}, bf16[128,256]{1,0:T(8,128)(2,1)S(1)}, bf16[128,256]{1,0:T(8,128)(2,1)S(1)}) conditional(s32[]{:T(128)} %clamp.27, (s32[2]{0:T(128)S(1)}, s32[311]{0:T(512)S(1)}, bf16[8,144,512]{2,1,0:T(8,128)(2,1)S(1)}, ...), branch_computations={%region_1.6_spmd, %region_6.11_spmd, %region_11.16_spmd} | conditional | flops 6561536 | bytes 96278752 | solution.py:347
  28.9 0.0 copy-start.8
  28.9 4.9 %partials.4 = bf16[2304,384]{1,0:T(8,128)(2,1)S(1)} custom-call(s32[2]{0:T(128)S(1)} %get-tuple-element.73.place, s32[311]{0:T(512)S(1)} %get-tuple-element.74.table, bf16[8,144,512]{2,1,0:T(8,128)(2,1)S(1)} %get-tuple-element.75.own.refs_6_, bf16[8,144,512]{2,1,0:T(8,128)(2,1)} %get-tuple-element.76.other, ...), custom_call_target="tpu_custom_call" | custom-call | tf_op jit(solution)/shard_map/cond/branch_1_fun/partials/pallas_call | solution.py:274
  33.8 0.0 copy-done.8
  33.8 0.0 copy-done.13
  33.8 0.0 copy-done.20
  33.9 26.0 %all_to_all.56 = bf16[4,576,384]{2,1,0:T(8,128)(2,1)S(1)} all-to-all(bf16[4,576,384]{2,1,0:T(8,128)(2,1)S(1)} %bitcast.24), channel_id=1, replica_groups=mesh['x'=4,'zh'=4,'core'=2,'zl'=2,'y'=4] {'x'}, dimensions={0} | all-to-all | bytes 3538944 | tf_op jit(solution)/shard_map/cond/branch_1_fun/all_to_all | solution.py:238
  59.9 0.2 convert_reduce_fusion.1
  60.1 0.1 abs_reduce_fusion.1
  60.2 0.1 multiply_convert_fusion.4
  60.3 0.1 pad_maximum_fusion.2
  60.5 18.1 %all_to_all.57 = f16[4,160,384]{2,1,0:T(8,128)(2,1)S(1)} all-to-all(f16[4,160,384]{2,1,0:T(8,128)(2,1)S(1)} %pad_maximum_fusion.2), channel_id=1, replica_groups=mesh['x'=4,'zh'=4,'core'=2,'zl'=2,'y'=4] {'zh'}, dimensions={0} | all-to-all | bytes 983040 | tf_op jit(solution)/shard_map/cond/branch_1_fun/all_to_all | solution.py:248
  78.6 0.1 convert_element_type.75
  78.7 0.1 fusion.3
  78.8 0.1 multiply_convert_fusion.7
  78.9 14.8 %all_to_all.58 = bf16[4,144,384]{2,1,0:T(8,128)(2,1)S(1)} all-to-all(bf16[4,144,384]{2,1,0:T(8,128)(2,1)S(1)} %broadcast_in_dim.17), channel_id=1, replica_groups=mesh['x'=4,'zh'=4,'core'=2,'zl'=2,'y'=4] {'zh'}, dimensions={0} | all-to-all | bytes 884736 | tf_op jit(solution)/shard_map/cond/branch_1_fun/all_to_all | solution.py:223
  93.7 0.3 collective-permute-start.7
  94.0 2.4 %collective-permute-start.8 = (bf16[576,384]{1,0:T(8,128)(2,1)S(1)}, bf16[576,384]{1,0:T(8,128)(2,1)S(1)}, u32[]{:S(2)}, u32[]{:S(2)}) collective-permute-start(bf16[576,384]{1,0:T(8,128)(2,1)S(1)} %bitcast.33), channel_id=1, source_target_pairs={{0,192},{64,0},{128,64},{192,128},{1,193},{65,1},{129,65},{193,129... | collective-permute-start | bytes 1327112 | tf_op jit(solution)/shard_map/cond/branch_1_fun/ppermute | solution.py:232
  96.4 5.7 %collective-permute-done.7 = bf16[576,384]{1,0:T(8,128)(2,1)S(1)} collective-permute-done((bf16[576,384]{1,0:T(8,128)(2,1)S(1)}, bf16[576,384]{1,0:T(8,128)(2,1)S(1)}, u32[]{:S(2)}, u32[]{:S(2)}) %collective-permute-start.7) | collective-permute-done | bytes 442400 | tf_op jit(solution)/shard_map/cond/branch_1_fun/ppermute | solution.py:232
  102.1 0.0 copy-start.14
  102.1 0.0 copy-start.21
  102.2 0.0 copy-start.25
  102.2 0.1 collective-permute-start.9
  102.3 0.0 collective-permute-done.8
  102.3 0.1 constant_dynamic-update-slice_fusion.4.refs_1_
  102.4 10.0 %collective-permute-start.12 = (bf16[1152,384]{1,0:T(8,128)(2,1)S(1)}, bf16[1152,384]{1,0:T(8,128)(2,1)S(1)}, u32[]{:S(2)}, u32[]{:S(2)}) collective-permute-start(bf16[1152,384]{1,0:T(8,128)(2,1)S(1)} %constant_dynamic-update-slice_fusion.4.refs_1_), channel_id=1, source_target_pairs={{0,8},{8,0},{1,9},{9,1},{2,10},{10,2},{3,11},{11,3},{4,12},{12,4},... | collective-permute-start | bytes 2654216 | tf_op jit(solution)/shard_map/cond/branch_1_fun/ppermute | solution.py:227
  112.5 3.0 %collective-permute-start.10 = (bf16[288,384]{1,0:T(8,128)(2,1)S(1)}, bf16[288,384]{1,0:T(8,128)(2,1)S(1)}, u32[]{:S(2)}, u32[]{:S(2)}) collective-permute-start(bf16[288,384]{1,0:T(8,128)(2,1)S(1)} %slice.100), channel_id=1, source_target_pairs={{0,192},{64,0},{128,64},{192,128},{1,193},{65,1},{129,65},{193,129... | collective-permute-start | bytes 663560 | tf_op jit(solution)/shard_map/cond/branch_1_fun/ppermute | solution.py:232
  115.5 0.3 collective-permute-start.11
  115.8 0.0 collective-permute-done.9
  115.8 4.5 %collective-permute-done.10 = bf16[288,384]{1,0:T(8,128)(2,1)S(1)} collective-permute-done((bf16[288,384]{1,0:T(8,128)(2,1)S(1)}, bf16[288,384]{1,0:T(8,128)(2,1)S(1)}, u32[]{:S(2)}, u32[]{:S(2)}) %collective-permute-start.10) | collective-permute-done | bytes 221216 | tf_op jit(solution)/shard_map/cond/branch_1_fun/ppermute | solution.py:232
  120.4 0.9 collective-permute-start.13
  121.3 0.0 collective-permute-done.11.refs_3_
  121.3 1.4 collective-permute-done.13.refs_5_
  122.7 0.0 collective-permute-done.12.refs_4_
  122.7 0.0 copy-done.14
  122.7 0.0 copy-done.21
  122.7 0.0 copy-done.25
  122.7 6.1 %row_grads.4 = bf16[1024,512]{1,0:T(8,128)(2,1)} custom-call(s32[2]{0:T(128)S(1)} %get-tuple-element.73.place, s32[311]{0:T(512)S(1)} %get-tuple-element.74.table, bf16[576,384]{1,0:T(8,128)(2,1)S(1)} %bitcast.35, bf16[1152,384]{1,0:T(8,128)(2,1)S(1)} %constant_dynamic-update-slice_fusion.4.refs_1_, ...), custom_call_target="tpu_custom_call" | custom-call | tf_op jit(solution)/shard_map/cond/branch_1_fun/row_grads/pallas_call | solution.py:285
  128.8 4.3 %all-to-all-start.7 = ((bf16[8,128,512]{2,1,0:T(8,128)(2,1)}), bf16[8,128,512]{2,1,0:T(8,128)(2,1)}, u32[]{:S(2)}, u32[]{:S(2)}) async-start(bf16[8,128,512]{2,1,0:T(8,128)(2,1)} %bitcast.7), calls=%async_computation.7 | async-start | bytes 2097152 | tf_op jit(solution)/shard_map/cond/branch_1_fun/all_to_all | solution.py:238
  133.0 10.1 %weight_grads.4 = (f32[256,1792]{1,0:T(8,128)}, f32[256,1792]{1,0:T(8,128)}, f32[1792,256]{1,0:T(8,128)}) custom-call(s32[2]{0:T(128)S(1)} %get-tuple-element.73.place, s32[311]{0:T(512)S(1)} %get-tuple-element.74.table, bf16[576,384]{1,0:T(8,128)(2,1)S(1)} %bitcast.36, bf16[1152,384]{1,0:T(8,128)(2,1)S(1)} %constant_dynamic-update-slice_fusion.4.refs_1_, ...), custom_call_target="tpu_custom_call" | custom-call | tf_op jit(solution)/shard_map/cond/branch_1_fun/weight_grads/pallas_call | solution.py:303
  143.1 4.9 %all-to-all-done.7 = bf16[8,128,512]{2,1,0:T(8,128)(2,1)} async-done(((bf16[8,128,512]{2,1,0:T(8,128)(2,1)}), bf16[8,128,512]{2,1,0:T(8,128)(2,1)}, u32[]{:S(2)}, u32[]{:S(2)}) %all-to-all-start.7) | async-done | bytes 1048608 | tf_op jit(solution)/shard_map/cond/branch_1_fun/all_to_all | solution.py:238
  148.0 1.4 reduce_sum.91
  149.9 0.0 copy-start.27
  149.9 0.0 copy-start.28
  149.9 0.6 copy-done.27
  150.5 0.0 copy-done.28
  (14 shorter events, 0.3 us)
Async XLA Ops:
  0.6 8.5 %copy-start.10 = (bf16[256,1792]{1,0:T(8,128)(2,1)S(1)}, bf16[256,1792]{1,0:T(8,128)(2,1)}, u32[]{:S(2)}) copy-start(bf16[256,1792]{1,0:T(8,128)(2,1)} %param.10) | copy-start | bytes 2752516
  0.6 9.6 %copy-start.17 = (bf16[256,1792]{1,0:T(8,128)(2,1)S(1)}, bf16[256,1792]{1,0:T(8,128)(2,1)}, u32[]{:S(2)}) copy-start(bf16[256,1792]{1,0:T(8,128)(2,1)} %param.11) | copy-start | bytes 2752516
  2.8 22.7 %all-to-all-start.12 = ((bf16[8,144,512]{2,1,0:T(8,128)(2,1)}), bf16[8,144,512]{2,1,0:T(8,128)(2,1)S(1)}, u32[]{:S(2)}, u32[]{:S(2)}) async-start(bf16[8,144,512]{2,1,0:T(8,128)(2,1)} %payload.1), calls=%async_computation.12 | async-start | bytes 2359296 | tf_op jit(solution)/shard_map/all_to_all | solution.py:339
  9.1 3.8 %collective-permute-start.21 = (bf16[256,1792]{1,0:T(8,128)(2,1)S(1)}, bf16[256,1792]{1,0:T(8,128)(2,1)}, u32[]{:S(2)}, u32[]{:S(2)}) collective-permute-start(bf16[256,1792]{1,0:T(8,128)(2,1)S(1)} %copy-done.10), channel_id=1, source_target_pairs={{0,8},{8,0},{1,9},{9,1},{2,10},{10,2},{3,11},{11,3},{4,12},{12,4},... | collective-permute-start | bytes 2752520 | tf_op jit(solution)/shard_map/ppermute | solution.py:227
  10.2 4.9 %collective-permute-start.22 = (bf16[256,1792]{1,0:T(8,128)(2,1)S(1)}, bf16[256,1792]{1,0:T(8,128)(2,1)}, u32[]{:S(2)}, u32[]{:S(2)}) collective-permute-start(bf16[256,1792]{1,0:T(8,128)(2,1)S(1)} %copy-done.17), channel_id=1, source_target_pairs={{0,8},{8,0},{1,9},{9,1},{2,10},{10,2},{3,11},{11,3},{4,12},{12,4},... | collective-permute-start | bytes 2752520 | tf_op jit(solution)/shard_map/ppermute | solution.py:227
  10.3 5.0 %collective-permute-start.23 = (bf16[1792,256]{1,0:T(8,128)(2,1)}, bf16[1792,256]{1,0:T(8,128)(2,1)}, u32[]{:S(2)}, u32[]{:S(2)}) collective-permute-start(bf16[1792,256]{1,0:T(8,128)(2,1)} %param.12), channel_id=1, source_target_pairs={{0,8},{8,0},{1,9},{9,1},{2,10},{10,2},{3,11},{11,3},{4,12},{12,4},... | collective-permute-start | bytes 2752520 | tf_op jit(solution)/shard_map/ppermute | solution.py:227
  25.5 3.5 %collective-permute-start.24 = (bf16[8,144,512]{2,1,0:T(8,128)(2,1)S(1)}, bf16[8,144,512]{2,1,0:T(8,128)(2,1)}, u32[]{:S(2)}, u32[]{:S(2)}) collective-permute-start(bf16[8,144,512]{2,1,0:T(8,128)(2,1)S(1)} %all-to-all-done.12), channel_id=1, source_target_pairs={{0,8},{8,0},{1,9},{9,1},{2,10},{10,2},{3,11},{11,3},{4,12},{12,4},... | collective-permute-start | bytes 3538952 | tf_op jit(solution)/shard_map/ppermute | solution.py:227
  28.9 4.9 %copy-start.8 = (bf16[8,144,512]{2,1,0:T(8,128)(2,1)}, bf16[8,144,512]{2,1,0:T(8,128)(2,1)S(1)}, u32[]{:S(2)}) copy-start(bf16[8,144,512]{2,1,0:T(8,128)(2,1)S(1)} %get-tuple-element.75.own.refs_6_) | copy-start | bytes 3538948 | tf_op jit(solution)/shard_map/cond
  28.9 4.9 %copy-start.13 = (bf16[256,1792]{1,0:T(8,128)(2,1)}, bf16[256,1792]{1,0:T(8,128)(2,1)S(1)}, u32[]{:S(2)}) copy-start(bf16[256,1792]{1,0:T(8,128)(2,1)S(1)} %get-tuple-element.77.gate_own.refs_6_) | copy-start | bytes 2752516 | tf_op jit(solution)/shard_map/cond
  28.9 4.9 %copy-start.20 = (bf16[256,1792]{1,0:T(8,128)(2,1)}, bf16[256,1792]{1,0:T(8,128)(2,1)S(1)}, u32[]{:S(2)}) copy-start(bf16[256,1792]{1,0:T(8,128)(2,1)S(1)} %get-tuple-element.79.up_own.refs_7_) | copy-start | bytes 2752516 | tf_op jit(solution)/shard_map/cond
  93.7 8.4 %collective-permute-start.7 = (bf16[576,384]{1,0:T(8,128)(2,1)S(1)}, bf16[576,384]{1,0:T(8,128)(2,1)S(1)}, u32[]{:S(2)}, u32[]{:S(2)}) collective-permute-start(bf16[576,384]{1,0:T(8,128)(2,1)S(1)} %bitcast.32), channel_id=1, source_target_pairs={{0,64},{64,128},{128,192},{192,0},{1,65},{65,129},{129,193},{193,1... | collective-permute-start | bytes 1327112 | tf_op jit(solution)/shard_map/cond/branch_1_fun/ppermute | solution.py:232
  94.0 8.3 %collective-permute-start.8 = (bf16[576,384]{1,0:T(8,128)(2,1)S(1)}, bf16[576,384]{1,0:T(8,128)(2,1)S(1)}, u32[]{:S(2)}, u32[]{:S(2)}) collective-permute-start(bf16[576,384]{1,0:T(8,128)(2,1)S(1)} %bitcast.33), channel_id=1, source_target_pairs={{0,192},{64,0},{128,64},{192,128},{1,193},{65,1},{129,65},{193,129... | collective-permute-start | bytes 1327112 | tf_op jit(solution)/shard_map/cond/branch_1_fun/ppermute | solution.py:232
  102.1 20.6 %copy-start.14 = (bf16[256,1792]{1,0:T(8,128)(2,1)S(1)}, bf16[256,1792]{1,0:T(8,128)(2,1)}, u32[]{:S(2)}) copy-start(bf16[256,1792]{1,0:T(8,128)(2,1)} %copy-done.13) | copy-start | bytes 2752516 | tf_op jit(solution)/shard_map/cond
  102.1 20.5 %copy-start.21 = (bf16[256,1792]{1,0:T(8,128)(2,1)S(1)}, bf16[256,1792]{1,0:T(8,128)(2,1)}, u32[]{:S(2)}) copy-start(bf16[256,1792]{1,0:T(8,128)(2,1)} %copy-done.20) | copy-start | bytes 2752516 | tf_op jit(solution)/shard_map/cond
  102.2 20.5 %copy-start.25 = (bf16[1792,256]{1,0:T(8,128)(2,1)S(1)}, bf16[1792,256]{1,0:T(8,128)(2,1)}, u32[]{:S(2)}) copy-start(bf16[1792,256]{1,0:T(8,128)(2,1)} %get-tuple-element.81.down_own.refs_8_) | copy-start | bytes 2752516 | tf_op jit(solution)/shard_map/cond
  102.2 13.6 %collective-permute-start.9 = (bf16[288,384]{1,0:T(8,128)(2,1)S(1)}, bf16[288,384]{1,0:T(8,128)(2,1)S(1)}, u32[]{:S(2)}, u32[]{:S(2)}) collective-permute-start(bf16[288,384]{1,0:T(8,128)(2,1)S(1)} %slice.99), channel_id=1, source_target_pairs={{0,64},{64,128},{128,192},{192,0},{1,65},{65,129},{129,193},{193,1... | collective-permute-start | bytes 663560 | tf_op jit(solution)/shard_map/cond/branch_1_fun/ppermute | solution.py:232
  102.4 20.3 %collective-permute-start.12 = (bf16[1152,384]{1,0:T(8,128)(2,1)S(1)}, bf16[1152,384]{1,0:T(8,128)(2,1)S(1)}, u32[]{:S(2)}, u32[]{:S(2)}) collective-permute-start(bf16[1152,384]{1,0:T(8,128)(2,1)S(1)} %constant_dynamic-update-slice_fusion.4.refs_1_), channel_id=1, source_target_pairs={{0,8},{8,0},{1,9},{9,1},{2,10},{10,2},{3,11},{11,3},{4,12},{12,4},... | collective-permute-start | bytes 2654216 | tf_op jit(solution)/shard_map/cond/branch_1_fun/ppermute | solution.py:227
  112.5 7.9 %collective-permute-start.10 = (bf16[288,384]{1,0:T(8,128)(2,1)S(1)}, bf16[288,384]{1,0:T(8,128)(2,1)S(1)}, u32[]{:S(2)}, u32[]{:S(2)}) collective-permute-start(bf16[288,384]{1,0:T(8,128)(2,1)S(1)} %slice.100), channel_id=1, source_target_pairs={{0,192},{64,0},{128,64},{192,128},{1,193},{65,1},{129,65},{193,129... | collective-permute-start | bytes 663560 | tf_op jit(solution)/shard_map/cond/branch_1_fun/ppermute | solution.py:232
  115.5 5.8 %collective-permute-start.11 = (bf16[576,384]{1,0:T(8,128)(2,1)S(1)}, bf16[576,384]{1,0:T(8,128)(2,1)S(1)}, u32[]{:S(2)}, u32[]{:S(2)}) collective-permute-start(bf16[576,384]{1,0:T(8,128)(2,1)S(1)} %bitcast.34), channel_id=1, source_target_pairs={{0,8},{8,0},{1,9},{9,1},{2,10},{10,2},{3,11},{11,3},{4,12},{12,4},... | collective-permute-start | bytes 1327112 | tf_op jit(solution)/shard_map/cond/branch_1_fun/ppermute | solution.py:227
  120.4 2.3 %collective-permute-start.13 = (bf16[576,384]{1,0:T(8,128)(2,1)S(1)}, bf16[576,384]{1,0:T(8,128)(2,1)S(1)}, u32[]{:S(2)}, u32[]{:S(2)}) collective-permute-start(bf16[576,384]{1,0:T(8,128)(2,1)S(1)} %constant_dynamic-update-slice_fusion.6.refs_2_), channel_id=1, source_target_pairs={{0,8},{8,0},{1,9},{9,1},{2,10},{10,2},{3,11},{11,3},{4,12},{12,4},... | collective-permute-start | bytes 1327112 | tf_op jit(solution)/shard_map/cond/branch_1_fun/ppermute | solution.py:227
  128.8 19.2 %all-to-all-start.7 = ((bf16[8,128,512]{2,1,0:T(8,128)(2,1)}), bf16[8,128,512]{2,1,0:T(8,128)(2,1)}, u32[]{:S(2)}, u32[]{:S(2)}) async-start(bf16[8,128,512]{2,1,0:T(8,128)(2,1)} %bitcast.7), calls=%async_computation.7 | async-start | bytes 2097152 | tf_op jit(solution)/shard_map/cond/branch_1_fun/all_to_all | solution.py:238
  149.9 0.6 copy-start.27
  149.9 0.6 copy-start.28
